TPU v7x, 512 devices: a whole 4x8x8 slice. The times are simulated.
512 devices in a mesh: row: 64 (over x, z, core), blk: 8 (over y).
Axes of the slice: x: 4, y: 8, z: 8, core: 2. Of those that a mesh axis runs over, the one named last changes fastest.
Arguments:
- factor_panel: bfloat16 [131072, 2, 2048], P('row', None, 'blk'), may hold values from -0.09375 to 0.09375
- right_side: float32 [256, 131072], P('blk', 'row'), may hold values from -6 to 6
- block_inverse: float32 [2, 2048, 2048], P(None, 'row', 'blk'), may hold values from -2 to 2, as said below
Outputs:
- solved: float32 [2, 256, 2048], P(None, 'blk', 'row')
- reduced_side: float32 [256, 131072], P('blk', 'row')
Inputs may be any that keep to these rules, and one draw needn't show every extreme that they name: block_inverse[k] is lower triangular with diagonal entries between 1 and 2.
All inputs are finite; a program needn't handle non-finite values.
Results may differ from a plain program's by a relative error of at most 0.015.
Values may be sent and summed in bfloat16 or wider, within the bound.
No kernel may reach another device: no remote copies, remote signals or barrier semaphores. Data moves between devices by JAX's collectives and lax.ppermute only.
A program may use at most 64 MiB of HBM per device.

v0:
```python
import jax
import jax.numpy as jnp
from jax import lax
from jax.sharding import PartitionSpec as P

STEPS = 2


def from_root(array, axis, root):
    mine = lax.axis_index(axis) == root
    return lax.psum(jnp.where(mine, array, jnp.zeros_like(array)), axis)


def local(factor_panel, right_side, block_inverse):
    blk_index = lax.axis_index("blk")
    row_index = lax.axis_index("row")
    dates_local = right_side.shape[0]
    width = factor_panel.shape[2]
    reduced_side = right_side
    outputs = []
    for section in range(STEPS):
        pivot_block = from_root(reduced_side, "row", section)
        pivot_cols = lax.all_to_all(pivot_block, "blk", split_axis=1, concat_axis=0, tiled=True)
        partial_value = jnp.dot(
            pivot_cols, block_inverse[section].T, precision=lax.Precision.HIGHEST
        )
        summed = lax.psum(partial_value, "blk")
        own_share = lax.dynamic_slice_in_dim(summed, blk_index * dates_local, dates_local, 0)
        gathered = lax.all_gather(summed.astype(jnp.bfloat16), "row", axis=1, tiled=True)
        group_cols = lax.dynamic_slice_in_dim(gathered, blk_index * width, width, 1)
        outputs.append(own_share)
        panel_now = factor_panel[:, section, :]
        update = lax.psum_scatter(
            lax.dot_general(
                group_cols, panel_now, (((1,), (1,)), ((), ())), preferred_element_type=jnp.float32
            ).astype(jnp.bfloat16),
            "blk",
            scatter_dimension=0,
            tiled=True,
        ).astype(jnp.float32)
        reduced_side = reduced_side - jnp.where(row_index > section, update, jnp.float32(0.0))
    return (jnp.stack(outputs), reduced_side)


def solution(mesh):
    placed = (P("row", None, "blk"), P("blk", "row"), P(None, "row", "blk"))
    return jax.shard_map(
        local,
        mesh=mesh,
        in_specs=placed,
        out_specs=(P(None, "blk", "row"), P("blk", "row")),
        check_vma=False,
    )
```

profile of v0, /device:TPU:4, one launch (start us, length us, event | category | flops | bytes accessed | tf_op | source)
XLA Modules:
  0.0 736.3 jit_solution(8217188928372666133)
XLA Ops:
  7.3 0.7 copy.22
  8.1 195.5 %all-reduce.3.cloned.1.call-done = f32[32,8,256]{2,0,1:T(8,128)} async-done(((f32[32,8,256]{2,0,1:T(8,128)}), f32[32,8,256]{2,0,1:T(8,128)}) %all-reduce.3.cloned.1.call-update) | async-done | bytes 262160 | tf_op jit(solution)/shard_map/psum | solution.py:11
  203.5 20.0 %all_to_all.38 = f32[32,8,256]{2,0,1:T(8,128)S(1)} all-to-all(f32[32,8,256]{2,0,1:T(8,128)} %all-reduce.3.cloned.1.call-done), channel_id=1, replica_groups=mesh['row'=64,'blk'=8] {'blk'}, dimensions={1} | all-to-all | bytes 524288 | tf_op jit(solution)/shard_map/all_to_all | solution.py:23
  223.5 1.1 fusion.5
  224.6 27.3 %psum.29 = f32[256,32]{0,1:T(8,128)S(1)} all-reduce(f32[256,32]{0,1:T(8,128)S(1)} %fusion.5), channel_id=1, replica_groups=mesh['row'=64,'blk'=8] {'blk'}, use_global_device_ids=true, to_apply=%region_1.2 | all-reduce | flops 8192 | bytes 65536 | tf_op jit(solution)/shard_map/psum | solution.py:27
  251.9 0.6 convert_element_type.18
  252.6 4.2 fusion.11
  256.8 71.7 %all-gather.3.cloned.1.call-done = bf16[256,2048]{0,1:T(8,128)(2,1)} async-done(((bf16[256,32]{0,1:T(8,128)(2,1)}), bf16[256,2048]{0,1:T(8,128)(2,1)}) %all-gather.3.cloned.1.call-update) | async-done | bytes 1048592 | tf_op jit(solution)/shard_map/all_gather | solution.py:29
  328.6 3.2 convolution_convert_fusion.1
  331.8 39.6 %reduce-scatter.3.cloned.1.call-done = bf16[32,2048]{1,0:T(8,128)(2,1)} async-done(((bf16[256,2048]{1,0:T(8,128)(2,1)}), bf16[32,2048]{1,0:T(8,128)(2,1)}) %reduce-scatter.3.cloned.1.call-update) | async-done | bytes 131088 | tf_op jit(solution)/shard_map/reduce_scatter | solution.py:33
  371.4 0.9 fusion
  372.4 0.7 copy.21
  373.2 188.1 %all-reduce.5.cloned.1.call-done = f32[32,8,256]{2,0,1:T(8,128)} async-done(((f32[32,8,256]{2,0,1:T(8,128)}), f32[32,8,256]{2,0,1:T(8,128)}) %all-reduce.5.cloned.1.call-update) | async-done | bytes 262160 | tf_op jit(solution)/shard_map/psum | solution.py:11
  561.3 20.0 %all_to_all.39 = f32[32,8,256]{2,0,1:T(8,128)S(1)} all-to-all(f32[32,8,256]{2,0,1:T(8,128)} %all-reduce.5.cloned.1.call-done), channel_id=1, replica_groups=mesh['row'=64,'blk'=8] {'blk'}, dimensions={1} | all-to-all | bytes 524288 | tf_op jit(solution)/shard_map/all_to_all | solution.py:23
  581.3 0.3 fusion.3
  581.6 27.3 %psum.31 = f32[256,32]{0,1:T(8,128)S(1)} all-reduce(f32[256,32]{0,1:T(8,128)S(1)} %fusion.3), channel_id=1, replica_groups=mesh['row'=64,'blk'=8] {'blk'}, use_global_device_ids=true, to_apply=%region_4.5 | all-reduce | flops 8192 | bytes 65536 | tf_op jit(solution)/shard_map/psum | solution.py:27
  608.9 0.6 convert_element_type.21
  609.6 75.9 %all-gather.5.cloned.1.call-done = bf16[256,2048]{0,1:T(8,128)(2,1)} async-done(((bf16[256,32]{0,1:T(8,128)(2,1)}), bf16[256,2048]{0,1:T(8,128)(2,1)}) %all-gather.5.cloned.1.call-update) | async-done | bytes 1048592 | tf_op jit(solution)/shard_map/all_gather | solution.py:29
  685.6 2.4 convolution_convert_fusion
  688.0 0.1 constant_dynamic-slice_fusion.1
  688.0 0.1 copy.6
  688.3 0.6 pad_maximum_fusion
  688.9 38.9 %reduce-scatter.5.cloned.1.call-done = bf16[32,2048]{1,0:T(8,128)(2,1)} async-done(((bf16[256,2048]{1,0:T(8,128)(2,1)}), bf16[32,2048]{1,0:T(8,128)(2,1)}) %reduce-scatter.5.cloned.1.call-update) | async-done | bytes 131088 | tf_op jit(solution)/shard_map/reduce_scatter | solution.py:33
  727.7 1.7 select_subtract_fusion
  (25 shorter events, 0.5 us)
Async XLA Ops:
  7.2 245.5 %copy-start = (bf16[2048,2,256]{2,1,0:T(2,128)(2,1)S(1)}, bf16[2048,2,256]{2,1,0:T(2,128)(2,1)}, u32[]{:S(2)}) copy-start(bf16[2048,2,256]{2,1,0:T(2,128)(2,1)} %param.3) | copy-start | bytes 6291460
  7.2 196.4 %all-reduce.3.cloned.1.call-start = ((), (), s32[]{:S(2)}) async-start(), calls=%async_computation.4 | async-start | bytes 524288 | tf_op jit(solution)/shard_map/psum | solution.py:11
  8.0 320.5 %all-gather.3.cloned.1.call-start = ((), (), s32[]{:S(2)}) async-start(), calls=%async_computation.5 | async-start | bytes 1064960 | tf_op jit(solution)/shard_map/all_gather | solution.py:29
  252.6 118.9 %reduce-scatter.3.cloned.1.call-start = ((), (), s32[]{:S(2)}) async-start(), calls=%async_computation.6 | async-start | bytes 1179648 | tf_op jit(solution)/shard_map/reduce_scatter | solution.py:33
  256.8 114.6 %copy-start.2 = (f32[32,2048]{1,0:T(8,128)S(1)}, f32[32,2048]{1,0:T(8,128)}, u32[]{:S(2)}) copy-start(f32[32,2048]{1,0:T(8,128)} %param.4) | copy-start | bytes 786436
  328.6 252.7 %copy-start.4 = (f32[2,32,256]{2,1,0:T(8,128)S(1)}, f32[2,32,256]{2,1,0:T(8,128)}, u32[]{:S(2)}) copy-start(f32[2,32,256]{2,1,0:T(8,128)} %param.5) | copy-start | bytes 196612
  331.7 353.8 %copy-start.1 = (bf16[2048,1,256]{2,1,0:T(2,128)(2,1)S(1)}, bf16[2048,1,256]{2,1,0:T(2,128)(2,1)}, u32[]{:S(2)}) copy-start(bf16[2048,1,256]{2,1,0:T(2,128)(2,1)} %get-tuple-element.2) | copy-start | bytes 3145732
  331.8 229.5 %all-reduce.5.cloned.1.call-start = ((), (), s32[]{:S(2)}) async-start(), calls=%async_computation.7 | async-start | bytes 524288 | tf_op jit(solution)/shard_map/psum | solution.py:11
  373.1 312.4 %all-gather.5.cloned.1.call-start = ((), (), s32[]{:S(2)}) async-start(), calls=%async_computation.8 | async-start | bytes 1064960 | tf_op jit(solution)/shard_map/all_gather | solution.py:29
  581.3 146.5 %copy-start.3 = (bf16[32,2048]{1,0:T(8,128)(2,1)S(1)}, bf16[32,2048]{1,0:T(8,128)(2,1)}, u32[]{:S(2)}) copy-start(bf16[32,2048]{1,0:T(8,128)(2,1)} %reduce-scatter.3.cloned.1.call-done) | copy-start | bytes 393220
  609.6 118.2 %reduce-scatter.5.cloned.1.call-start = ((), (), s32[]{:S(2)}) async-start(), calls=%async_computation.9 | async-start | bytes 1179648 | tf_op jit(solution)/shard_map/reduce_scatter | solution.py:33
Sparse Core Ops, SparseCore 0:
  12.0 191.4 all-reduce.2
  252.7 75.8 all-gather.2
  331.9 39.4 reduce-scatter.2
  375.3 185.9 all-reduce.4
  609.7 75.8 all-gather.4
  688.2 39.4 reduce-scatter.4
where the time goes:
time: 737 us; the launch traced here: 736 us
  waiting for transfers between devices  610 us (83%)
  blocking collectives  94.6 us (13%)
  between operations  14.2 us (2%)
    psum x2, waiting for transfers between devices, from_root(): return lax.psum(jnp.where(mine, array, jnp.zeros_like(array)), axis)  384 us
    all_gather x2, waiting for transfers between devices, local(): lax.all_gather(summed.astype(jnp.bfloat16), 'row', axis=1, tiled=True)  148 us
    reduce_scatter x2, waiting for transfers between devices, local(): lax.psum_scatter(lax.dot_general(group_cols, panel_now, (((1,), (1,)), ((...  78.4 us
    psum x2, blocking collectives, local(): summed = lax.psum(partial_value, 'blk')  54.6 us
    all_to_all x2, blocking collectives, local(): lax.all_to_all(pivot_block, 'blk', split_axis=1, concat_axis=0, tiled=True)  40 us
  transfers between devices with their start and end apart: 6, of which 6 were waited for; matrix products, arithmetic and copies ran while one was open for 1% of the time, Pallas kernels for 0%

commit v1 on v0

--- a/solution.py
+++ b/solution.py
@@ -26,7 +26,12 @@
         )
         summed = lax.psum(partial_value, "blk")
         own_share = lax.dynamic_slice_in_dim(summed, blk_index * dates_local, dates_local, 0)
-        gathered = lax.all_gather(summed.astype(jnp.bfloat16), "row", axis=1, tiled=True)
+        gathered = jnp.concatenate(
+            lax.all_to_all(
+                jnp.stack([summed.astype(jnp.bfloat16)] * lax.axis_size("row")), "row", 0, 0
+            ),
+            axis=1,
+        )
         group_cols = lax.dynamic_slice_in_dim(gathered, blk_index * width, width, 1)
         outputs.append(own_share)
         panel_now = factor_panel[:, section, :]

time: 737 us -> 644 us (0.87)
  the two profiles are of different devices: /device:TPU:4 before, /device:TPU:2 now
where the time goes in v1:
time: 644 us; the launch traced here: 643 us
  waiting for transfers between devices  480 us (75%)
  blocking collectives  127 us (20%)
  between operations  13.9 us (2%)
  local copies, waits for them, and re-layouts  7.21 us (1%)
    psum x2, waiting for transfers between devices, from_root(): return lax.psum(jnp.where(mine, array, jnp.zeros_like(array)), axis)  385 us
    reduce_scatter x2, waiting for transfers between devices, local(): lax.psum_scatter(lax.dot_general(group_cols, panel_now, (((1,), (1,)), ((...  72.1 us
    psum x2, blocking collectives, local(): summed = lax.psum(partial_value, 'blk')  54.6 us
    all_to_all x2, blocking collectives, local(): lax.all_to_all(pivot_block, 'blk', split_axis=1, concat_axis=0, tiled=True)  40 us
    all_to_all x1, blocking collectives, local(): lax.all_to_all(jnp.stack([summed.astype(jnp.bfloat16)] * lax.axis_size('r...  32.4 us
    all_to_all x1, waiting for transfers between devices, local(): lax.all_to_all(jnp.stack([summed.astype(jnp.bfloat16)] * lax.axis_size('r...  22.7 us
  transfers between devices with their start and end apart: 5, of which 5 were waited for; matrix products, arithmetic and copies ran while one was open for 1% of the time, Pallas kernels for 0%

profile of v1, /device:TPU:2, one launch (start us, length us, event | category | flops | bytes accessed | tf_op | source)
XLA Modules:
  0.0 643.3 jit_solution(10224945748858545569)
XLA Ops:
  7.3 0.7 copy.24
  8.0 196.3 %all-reduce.3.cloned.1.call-done = f32[32,8,256]{2,0,1:T(8,128)} async-done(((f32[32,8,256]{2,0,1:T(8,128)}), f32[32,8,256]{2,0,1:T(8,128)}) %all-reduce.3.cloned.1.call-update) | async-done | bytes 262160 | tf_op jit(solution)/shard_map/psum | solution.py:11
  204.3 20.0 %all_to_all.48 = f32[32,8,256]{2,0,1:T(8,128)S(1)} all-to-all(f32[32,8,256]{2,0,1:T(8,128)} %all-reduce.3.cloned.1.call-done), channel_id=1, replica_groups=mesh['row'=64,'blk'=8] {'blk'}, dimensions={1} | all-to-all | bytes 524288 | tf_op jit(solution)/shard_map/all_to_all | solution.py:23
  224.3 1.1 fusion.5
  225.4 27.3 %psum.29 = f32[256,32]{0,1:T(8,128)S(1)} all-reduce(f32[256,32]{0,1:T(8,128)S(1)} %fusion.5), channel_id=1, replica_groups=mesh['row'=64,'blk'=8] {'blk'}, use_global_device_ids=true, to_apply=%region_1.2 | all-reduce | flops 8192 | bytes 65536 | tf_op jit(solution)/shard_map/psum | solution.py:27
  252.7 1.1 stack.11
  253.8 5.6 all-to-all-start.1
  259.5 4.2 fusion.11
  263.7 22.7 %all-to-all-done.1 = bf16[64,256,32]{1,2,0:T(8,128)(2,1)S(1)} async-done(((bf16[64,256,32]{1,2,0:T(8,128)(2,1)}), bf16[64,256,32]{1,2,0:T(8,128)(2,1)S(1)}, u32[]{:S(2)}, u32[]{:S(2)}) %all-to-all-start.1) | async-done | bytes 1048608 | tf_op jit(solution)/shard_map/all_to_all | solution.py:30
  286.4 3.1 convolution_convert_fusion.1
  289.6 36.5 %reduce-scatter.3.cloned.1.call-done = bf16[32,2048]{1,0:T(8,128)(2,1)} async-done(((bf16[256,2048]{1,0:T(8,128)(2,1)}), bf16[32,2048]{1,0:T(8,128)(2,1)}) %reduce-scatter.3.cloned.1.call-update) | async-done | bytes 131088 | tf_op jit(solution)/shard_map/reduce_scatter | solution.py:38
  326.0 0.9 fusion
  327.0 0.7 copy.23
  327.8 189.1 %all-reduce.5.cloned.1.call-done = f32[32,8,256]{2,0,1:T(8,128)} async-done(((f32[32,8,256]{2,0,1:T(8,128)}), f32[32,8,256]{2,0,1:T(8,128)}) %all-reduce.5.cloned.1.call-update) | async-done | bytes 262160 | tf_op jit(solution)/shard_map/psum | solution.py:11
  516.9 20.0 %all_to_all.49 = f32[32,8,256]{2,0,1:T(8,128)S(1)} all-to-all(f32[32,8,256]{2,0,1:T(8,128)} %all-reduce.5.cloned.1.call-done), channel_id=1, replica_groups=mesh['row'=64,'blk'=8] {'blk'}, dimensions={1} | all-to-all | bytes 524288 | tf_op jit(solution)/shard_map/all_to_all | solution.py:23
  536.9 0.3 fusion.3
  537.2 27.3 %psum.31 = f32[256,32]{0,1:T(8,128)S(1)} all-reduce(f32[256,32]{0,1:T(8,128)S(1)} %fusion.3), channel_id=1, replica_groups=mesh['row'=64,'blk'=8] {'blk'}, use_global_device_ids=true, to_apply=%region_4.5 | all-reduce | flops 8192 | bytes 65536 | tf_op jit(solution)/shard_map/psum | solution.py:27
  564.5 0.1 stack.14
  564.7 32.4 %all_to_all.50 = bf16[64,256,32]{1,2,0:T(8,128)(2,1)S(1)} all-to-all(bf16[64,256,32]{1,2,0:T(8,128)(2,1)S(1)} %stack.14), channel_id=1, replica_groups=mesh['row'=64,'blk'=8] {'row'}, dimensions={0} | all-to-all | bytes 2097152 | tf_op jit(solution)/shard_map/all_to_all | solution.py:30
  597.0 1.5 convolution_convert_fusion
  598.6 0.1 constant_dynamic-slice_fusion.1
  598.9 0.6 pad_maximum_fusion
  599.5 35.6 %reduce-scatter.5.cloned.1.call-done = bf16[32,2048]{1,0:T(8,128)(2,1)} async-done(((bf16[256,2048]{1,0:T(8,128)(2,1)}), bf16[32,2048]{1,0:T(8,128)(2,1)}) %reduce-scatter.5.cloned.1.call-update) | async-done | bytes 131088 | tf_op jit(solution)/shard_map/reduce_scatter | solution.py:38
  635.1 1.7 select_subtract_fusion
  (24 shorter events, 0.5 us)
Async XLA Ops:
  7.2 197.1 %all-reduce.3.cloned.1.call-start = ((), (), s32[]{:S(2)}) async-start(), calls=%async_computation.6 | async-start | bytes 524288 | tf_op jit(solution)/shard_map/psum | solution.py:11
  8.0 251.5 %copy-start = (bf16[2048,2,256]{2,1,0:T(2,128)(2,1)S(1)}, bf16[2048,2,256]{2,1,0:T(2,128)(2,1)}, u32[]{:S(2)}) copy-start(bf16[2048,2,256]{2,1,0:T(2,128)(2,1)} %param.3) | copy-start | bytes 6291460
  253.8 32.6 %all-to-all-start.1 = ((bf16[64,256,32]{1,2,0:T(8,128)(2,1)}), bf16[64,256,32]{1,2,0:T(8,128)(2,1)S(1)}, u32[]{:S(2)}, u32[]{:S(2)}) async-start(bf16[64,256,32]{1,2,0:T(8,128)(2,1)} %stack.11), calls=%async_computation.1 | async-start | bytes 2097152 | tf_op jit(solution)/shard_map/all_to_all | solution.py:30
  259.4 66.6 %reduce-scatter.3.cloned.1.call-start = ((), (), s32[]{:S(2)}) async-start(), calls=%async_computation.7 | async-start | bytes 1179648 | tf_op jit(solution)/shard_map/reduce_scatter | solution.py:38
  263.7 62.3 %copy-start.2 = (f32[32,2048]{1,0:T(8,128)S(1)}, f32[32,2048]{1,0:T(8,128)}, u32[]{:S(2)}) copy-start(f32[32,2048]{1,0:T(8,128)} %param.4) | copy-start | bytes 786436
  286.4 250.5 %copy-start.4 = (f32[2,32,256]{2,1,0:T(8,128)S(1)}, f32[2,32,256]{2,1,0:T(8,128)}, u32[]{:S(2)}) copy-start(f32[2,32,256]{2,1,0:T(8,128)} %param.5) | copy-start | bytes 196612
  289.5 227.4 %all-reduce.5.cloned.1.call-start = ((), (), s32[]{:S(2)}) async-start(), calls=%async_computation.8 | async-start | bytes 524288 | tf_op jit(solution)/shard_map/psum | solution.py:11
  327.7 269.3 %copy-start.1 = (bf16[2048,1,256]{2,1,0:T(2,128)(2,1)S(1)}, bf16[2048,1,256]{2,1,0:T(2,128)(2,1)}, u32[]{:S(2)}) copy-start(bf16[2048,1,256]{2,1,0:T(2,128)(2,1)} %get-tuple-element.2) | copy-start | bytes 3145732
  327.7 307.3 %reduce-scatter.5.cloned.1.call-start = ((), (), s32[]{:S(2)}) async-start(), calls=%async_computation.9 | async-start | bytes 1179648 | tf_op jit(solution)/shard_map/reduce_scatter | solution.py:38
  597.0 38.1 %copy-start.3 = (bf16[32,2048]{1,0:T(8,128)(2,1)S(1)}, bf16[32,2048]{1,0:T(8,128)(2,1)}, u32[]{:S(2)}) copy-start(bf16[32,2048]{1,0:T(8,128)(2,1)} %reduce-scatter.3.cloned.1.call-done) | copy-start | bytes 393220
Sparse Core Ops, SparseCore 0:
  12.0 192.2 all-reduce.2
  289.6 36.3 reduce-scatter.2
  330.1 186.7 all-reduce.4
  598.7 36.3 reduce-scatter.4

commit v2 on v0

--- a/solution.py
+++ b/solution.py
@@ -8,7 +8,7 @@
 
 def from_root(array, axis, root):
     mine = lax.axis_index(axis) == root
-    return lax.psum(jnp.where(mine, array, jnp.zeros_like(array)), axis)
+    return jnp.sum(lax.all_gather(jnp.where(mine, array, jnp.zeros_like(array)), axis), axis=0)
 
 
 def local(factor_panel, right_side, block_inverse):

time: 737 us -> 584 us (0.79)
  waiting for transfers between devices: 610 us -> 446 us
  other arithmetic: 4.48 us -> 19.4 us
    psum x2 -> x0, waiting for transfers between devices: 384 us -> none  [from_root(): return lax.psum(jnp.where(mine, array, jnp.zeros_like(array)), axis)]
    all_gather x0 -> x2, waiting for transfers between devices: none -> 218 us  [from_root(): lax.all_gather(jnp.where(mine, array, jnp.zeros_like(array)), axis)]
    reduce_sum x0 -> x2, other arithmetic: none -> 13.6 us  [from_root(): jnp.sum(lax.all_gather(jnp.where(mine, array, jnp.zeros_like(array)), axi...]
where the time goes in v2:
time: 584 us; the launch traced here: 583 us
  waiting for transfers between devices  446 us (76%)
  blocking collectives  92.6 us (16%)
  other arithmetic  19.4 us (3%)
  between operations  14.2 us (2%)
  matrix products  6.27 us (1%)
    all_gather x2, waiting for transfers between devices, from_root(): lax.all_gather(jnp.where(mine, array, jnp.zeros_like(array)), axis)  218 us
    all_gather x2, waiting for transfers between devices, local(): lax.all_gather(summed.astype(jnp.bfloat16), 'row', axis=1, tiled=True)  150 us
    reduce_scatter x2, waiting for transfers between devices, local(): lax.psum_scatter(lax.dot_general(group_cols, panel_now, (((1,), (1,)), ((...  78.3 us
    psum x2, blocking collectives, local(): summed = lax.psum(partial_value, 'blk')  55 us
    all_to_all x2, blocking collectives, local(): lax.all_to_all(pivot_block, 'blk', split_axis=1, concat_axis=0, tiled=True)  37.7 us
    reduce_sum x2, other arithmetic, from_root(): jnp.sum(lax.all_gather(jnp.where(mine, array, jnp.zeros_like(array)), axi...  13.6 us
  transfers between devices with their start and end apart: 6, of which 6 were waited for; matrix products, arithmetic and copies ran while one was open for 1% of the time, Pallas kernels for 0%

profile of v2, /device:TPU:4, one launch (start us, length us, event | category | flops | bytes accessed | tf_op | source)
XLA Modules:
  0.0 583.5 jit_solution(17191434402451414825)
XLA Ops:
  7.2 0.7 broadcast_select_fusion
  8.0 112.4 %all-gather.11.cloned.1.call-done = f32[2048,2048]{1,0:T(8,128)} async-done(((f32[32,2048]{1,0:T(8,128)}), f32[2048,2048]{1,0:T(8,128)}) %all-gather.11.cloned.1.call-update) | async-done | bytes 16777232 | tf_op jit(solution)/shard_map/all_gather | solution.py:11
  120.4 6.8 %reduce_sum.18 = f32[32,2048]{1,0:T(8,128)S(1)} reduce(f32[64,32,2048]{2,1,0:T(8,128)} %bitcast.33, f32[]{:T(128)} %constant.5.clone.1), dimensions={0}, to_apply=%region_0.1 | reduce | flops 4128768 | bytes 17039364 | tf_op jit(solution)/shard_map/reduce_sum | solution.py:11
  127.3 18.8 %all_to_all.38 = f32[32,8,256]{2,0,1:T(8,128)S(1)} all-to-all(f32[32,8,256]{2,0,1:T(8,128)S(1)} %bitcast.38), channel_id=1, replica_groups=mesh['row'=64,'blk'=8] {'blk'}, dimensions={1} | all-to-all | bytes 524288 | tf_op jit(solution)/shard_map/all_to_all | solution.py:23
  146.1 0.3 fusion.5
  146.4 27.5 %psum.14 = f32[256,32]{0,1:T(8,128)S(1)} all-reduce(f32[256,32]{0,1:T(8,128)S(1)} %fusion.5), channel_id=1, replica_groups=mesh['row'=64,'blk'=8] {'blk'}, use_global_device_ids=true, to_apply=%region_1.2 | all-reduce | flops 8192 | bytes 65536 | tf_op jit(solution)/shard_map/psum | solution.py:27
  173.9 0.6 convert_element_type.18
  174.6 4.3 fusion.11
  178.9 72.9 %all-gather.7.cloned.1.call-done = bf16[256,2048]{0,1:T(8,128)(2,1)} async-done(((bf16[256,32]{0,1:T(8,128)(2,1)}), bf16[256,2048]{0,1:T(8,128)(2,1)}) %all-gather.7.cloned.1.call-update) | async-done | bytes 1048592 | tf_op jit(solution)/shard_map/all_gather | solution.py:29
  251.8 3.1 convolution_convert_fusion.1
  255.1 39.5 %reduce-scatter.3.cloned.1.call-done = bf16[32,2048]{1,0:T(8,128)(2,1)} async-done(((bf16[256,2048]{1,0:T(8,128)(2,1)}), bf16[32,2048]{1,0:T(8,128)(2,1)}) %reduce-scatter.3.cloned.1.call-update) | async-done | bytes 131088 | tf_op jit(solution)/shard_map/reduce_scatter | solution.py:33
  294.6 1.6 fusion
  296.3 105.1 %all-gather.13.cloned.1.call-done = f32[2048,2048]{1,0:T(8,128)} async-done(((f32[32,2048]{1,0:T(8,128)}), f32[2048,2048]{1,0:T(8,128)}) %all-gather.13.cloned.1.call-update) | async-done | bytes 16777232 | tf_op jit(solution)/shard_map/all_gather | solution.py:11
  401.4 6.8 %reduce_sum.19 = f32[32,2048]{1,0:T(8,128)S(1)} reduce(f32[64,32,2048]{2,1,0:T(8,128)} %bitcast.32, f32[]{:T(128)} %constant.5.clone.1), dimensions={0}, to_apply=%region_3.4 | reduce | flops 4128768 | bytes 17039364 | tf_op jit(solution)/shard_map/reduce_sum | solution.py:11
  408.2 18.8 %all_to_all.39 = f32[32,8,256]{2,0,1:T(8,128)S(1)} all-to-all(f32[32,8,256]{2,0,1:T(8,128)S(1)} %bitcast.39), channel_id=1, replica_groups=mesh['row'=64,'blk'=8] {'blk'}, dimensions={1} | all-to-all | bytes 524288 | tf_op jit(solution)/shard_map/all_to_all | solution.py:23
  427.0 0.3 fusion.3
  427.4 27.5 %psum.15 = f32[256,32]{0,1:T(8,128)S(1)} all-reduce(f32[256,32]{0,1:T(8,128)S(1)} %fusion.3), channel_id=1, replica_groups=mesh['row'=64,'blk'=8] {'blk'}, use_global_device_ids=true, to_apply=%region_4.5 | all-reduce | flops 8192 | bytes 65536 | tf_op jit(solution)/shard_map/psum | solution.py:27
  454.9 0.6 convert_element_type.21
  455.6 77.2 %all-gather.9.cloned.1.call-done = bf16[256,2048]{0,1:T(8,128)(2,1)} async-done(((bf16[256,32]{0,1:T(8,128)(2,1)}), bf16[256,2048]{0,1:T(8,128)(2,1)}) %all-gather.9.cloned.1.call-update) | async-done | bytes 1048592 | tf_op jit(solution)/shard_map/all_gather | solution.py:29
  532.8 2.4 convolution_convert_fusion
  535.3 0.1 constant_dynamic-slice_fusion.1
  535.6 0.6 pad_maximum_fusion
  536.2 38.8 %reduce-scatter.5.cloned.1.call-done = bf16[32,2048]{1,0:T(8,128)(2,1)} async-done(((bf16[256,2048]{1,0:T(8,128)(2,1)}), bf16[32,2048]{1,0:T(8,128)(2,1)}) %reduce-scatter.5.cloned.1.call-update) | async-done | bytes 131088 | tf_op jit(solution)/shard_map/reduce_scatter | solution.py:33
  575.0 1.7 select_subtract_fusion
  (27 shorter events, 0.6 us)
Async XLA Ops:
  7.2 113.3 %all-gather.11.cloned.1.call-start = ((), (), s32[]{:S(2)}) async-start(), calls=%async_computation.8 | async-start | bytes 17039360 | tf_op jit(solution)/shard_map/all_gather | solution.py:11
  8.0 243.8 %all-gather.7.cloned.1.call-start = ((), (), s32[]{:S(2)}) async-start(), calls=%async_computation.4 | async-start | bytes 1064960 | tf_op jit(solution)/shard_map/all_gather | solution.py:29
  120.4 25.6 %copy-start.4 = (f32[2,32,256]{2,1,0:T(8,128)S(1)}, f32[2,32,256]{2,1,0:T(8,128)}, u32[]{:S(2)}) copy-start(f32[2,32,256]{2,1,0:T(8,128)} %param.5) | copy-start | bytes 196612
  120.4 54.2 %copy-start = (bf16[2048,2,256]{2,1,0:T(2,128)(2,1)S(1)}, bf16[2048,2,256]{2,1,0:T(2,128)(2,1)}, u32[]{:S(2)}) copy-start(bf16[2048,2,256]{2,1,0:T(2,128)(2,1)} %param.3) | copy-start | bytes 6291460
  174.5 120.0 %reduce-scatter.3.cloned.1.call-start = ((), (), s32[]{:S(2)}) async-start(), calls=%async_computation.5 | async-start | bytes 1179648 | tf_op jit(solution)/shard_map/reduce_scatter | solution.py:33
  178.9 115.7 %copy-start.2 = (f32[32,2048]{1,0:T(8,128)S(1)}, f32[32,2048]{1,0:T(8,128)}, u32[]{:S(2)}) copy-start(f32[32,2048]{1,0:T(8,128)} %param.4) | copy-start | bytes 786436
  255.0 146.4 %all-gather.13.cloned.1.call-start = ((), (), s32[]{:S(2)}) async-start(), calls=%async_computation.9 | async-start | bytes 17039360 | tf_op jit(solution)/shard_map/all_gather | solution.py:11
  296.2 236.5 %all-gather.9.cloned.1.call-start = ((), (), s32[]{:S(2)}) async-start(), calls=%async_computation.6 | async-start | bytes 1064960 | tf_op jit(solution)/shard_map/all_gather | solution.py:29
  401.4 131.4 %copy-start.1 = (bf16[2048,1,256]{2,1,0:T(2,128)(2,1)S(1)}, bf16[2048,1,256]{2,1,0:T(2,128)(2,1)}, u32[]{:S(2)}) copy-start(bf16[2048,1,256]{2,1,0:T(2,128)(2,1)} %get-tuple-element.2) | copy-start | bytes 3145732
  427.0 147.9 %copy-start.3 = (bf16[32,2048]{1,0:T(8,128)(2,1)S(1)}, bf16[32,2048]{1,0:T(8,128)(2,1)}, u32[]{:S(2)}) copy-start(bf16[32,2048]{1,0:T(8,128)(2,1)} %reduce-scatter.3.cloned.1.call-done) | copy-start | bytes 393220
  455.5 119.5 %reduce-scatter.5.cloned.1.call-start = ((), (), s32[]{:S(2)}) async-start(), calls=%async_computation.7 | async-start | bytes 1179648 | tf_op jit(solution)/shard_map/reduce_scatter | solution.py:33
Sparse Core Ops, SparseCore 0:
  11.9 108.4 all-gather.10
  174.7 77.1 all-gather.6
  255.1 39.4 reduce-scatter.2
  298.4 103.0 all-gather.12
  455.6 77.1 all-gather.8
  535.5 39.4 reduce-scatter.4
